TPU v7x, 128 devices: a whole 4x4x4 slice. The times are simulated.
128 devices in a mesh: ctx: 16 (over y, z), seq: 8 (over x, core).
Axes of the slice: x: 4, y: 4, z: 4, core: 2. Of those that a mesh axis runs over, the one named last changes fastest.
Arguments:
- mixer_input: bfloat16 [16384, 16384], P(('seq', 'ctx')), may hold values from -6 to 6
- step_raw: bfloat16 [16384, 256], P(('seq', 'ctx')), may hold values from -7 to 2.5
- b_proj: bfloat16 [16384, 2048], P(('seq', 'ctx')), may hold values from -3 to 3
- c_proj: bfloat16 [16384, 2048], P(('seq', 'ctx')), may hold values from -0.375 to 0.375
- step_bias: float32 [256], replicated, may hold values from -2 to 2
- decay_log: float32 [256], replicated, may hold values from -3.9 to -2.5
- skip_gain: float32 [256], replicated, may hold values from 0.5 to 1.5
Outputs:
- mixer_output: bfloat16 [16384, 16384], P(('seq', 'ctx'))
All inputs are finite; a program needn't handle non-finite values.
Results may differ from a plain program's by a relative error of at most 0.0044.
Values may be sent and summed in bfloat16 or wider, within the bound.
A program may use at most 192 MiB of HBM per device.

v0:
```python
import jax
import jax.numpy as jnp
from jax import lax
from jax.sharding import PartitionSpec as P

P_SIZE = 64
N = 256
G = 8
Q = 128


def from_behind(value, axis, steps):
    count = lax.axis_size(axis)
    leading, last = (max(0, -steps), min(count, count - steps))
    return lax.ppermute(value, axis, [(source, source + steps) for source in range(leading, last)])


def span_parts(inputs_x, step_size, neg_rate, b_span, c_span, groups):
    count, length, heads = step_size.shape
    share = heads // groups
    cum = jnp.cumsum(step_size * neg_rate, axis=1)
    inner = jnp.einsum("cign,cjgn->cgij", c_span, b_span, preferred_element_type=jnp.float32)
    cum_t = jnp.transpose(cum, (0, 2, 1))
    diff = cum_t[:, :, :, None] - cum_t[:, :, None, :]
    rows = lax.broadcasted_iota(jnp.int32, (length, length), 0)
    cols = lax.broadcasted_iota(jnp.int32, (length, length), 1)
    decay = jnp.exp(jnp.where(rows >= cols, diff, -jnp.inf))
    step_t = jnp.transpose(step_size, (0, 2, 1))
    scores = (
        inner[:, :, None]
        * decay.reshape(count, groups, share, length, length)
        * step_t.reshape(count, groups, share, 1, length)
    )
    scores = scores.reshape(count, heads, length, length).astype(jnp.bfloat16)
    diag = jnp.einsum("chij,cjhp->cihp", scores, inputs_x, preferred_element_type=jnp.float32)
    tail = jnp.exp(cum[:, -1:, :] - cum) * step_size
    weighted = b_span[:, :, :, None, :] * tail.reshape(count, length, groups, share, 1)
    weighted = weighted.reshape(count, length, heads, b_span.shape[3]).astype(jnp.bfloat16)
    states = jnp.einsum("cjhn,cjhp->chnp", weighted, inputs_x, preferred_element_type=jnp.float32)
    return (diag, states, cum)


def off_part(c_span, entry_bf, cum, groups):
    count, length, heads = cum.shape
    share = heads // groups
    width = entry_bf.shape[2]
    depth = entry_bf.shape[3]
    outer = jnp.einsum(
        "cign,cgknp->cigkp",
        c_span,
        entry_bf.reshape(count, groups, share, width, depth),
        preferred_element_type=jnp.float32,
    )
    return outer.reshape(count, length, heads, depth) * jnp.exp(cum)[..., None]


def apply_segmented_scan(states, logs):

    def advance(carry, items):
        factor, piece = items
        return (factor[:, None, None] * carry + piece, carry)

    final, entry_rows = lax.scan(advance, jnp.zeros_like(states[0]), (jnp.exp(logs), states))
    running = jnp.cumsum(logs, axis=0)
    leading_state = jnp.exp(running - logs)
    return (entry_rows, final, leading_state, running[-1])


def pass_blocks(factor, state):

    def forward(turn_index, incoming):
        return from_behind(factor[:, None, None] * incoming + state, "seq", 1)

    return lax.fori_loop(0, lax.axis_size("seq") - 1, forward, jnp.zeros_like(state))


def body(mixer_input, step_raw, b_proj, c_proj, step_bias, decay_log, skip_gain):
    ctx_count = lax.axis_size("ctx")
    tok_rows = mixer_input.shape[0]
    heads = step_raw.shape[1]
    neg_rate = -jnp.exp(decay_log)
    local = heads // ctx_count
    repeat = ctx_count // G
    paired = jnp.concatenate(
        (b_proj.reshape(tok_rows, G, 1, N), c_proj.reshape(tok_rows, G, 1, N)), axis=3
    )
    paired = jnp.broadcast_to(paired, (tok_rows, G, repeat, 2 * N)).reshape(
        tok_rows, ctx_count * 2 * N
    )
    block_x, block_step, block_pair = (
        lax.all_to_all(mixer_input, "ctx", split_axis=1, concat_axis=0, tiled=True),
        lax.all_to_all(step_raw, "ctx", split_axis=1, concat_axis=0, tiled=True),
        lax.all_to_all(paired, "ctx", split_axis=1, concat_axis=0, tiled=True),
    )
    block = block_x.shape[0]
    count = block // Q
    start = lax.axis_index("ctx") * local
    bias_local = lax.dynamic_slice_in_dim(step_bias, start, local)
    rate_local = lax.dynamic_slice_in_dim(neg_rate, start, local)
    gain_local = lax.dynamic_slice_in_dim(skip_gain, start, local)
    step_size = jax.nn.softplus(block_step.astype(jnp.float32) + bias_local).reshape(
        count, Q, local
    )
    inputs_x = block_x.reshape(count, Q, local, P_SIZE)
    b_span = block_pair[:, :N].reshape(count, Q, 1, N)
    c_span = block_pair[:, N:].reshape(count, Q, 1, N)
    diag, states, cum = span_parts(inputs_x, step_size, rate_local, b_span, c_span, 1)
    entry_rows, final, leading_state, whole = apply_segmented_scan(states, cum[:, -1, :])
    incoming = pass_blocks(jnp.exp(whole), final)
    entry_bf = (entry_rows + leading_state[:, :, None, None] * incoming[None]).astype(jnp.bfloat16)
    off = off_part(c_span, entry_bf, cum, 1)
    result = (diag + off + gain_local[:, None] * inputs_x.astype(jnp.float32)).astype(jnp.bfloat16)
    return lax.all_to_all(
        result.reshape(block, local * P_SIZE), "ctx", split_axis=0, concat_axis=1, tiled=True
    )


def solution(mesh):
    return jax.shard_map(
        body,
        mesh=mesh,
        in_specs=(
            P(("seq", "ctx"), None),
            P(("seq", "ctx"), None),
            P(("seq", "ctx"), None),
            P(("seq", "ctx"), None),
            P(),
            P(),
            P(),
        ),
        out_specs=P(("seq", "ctx"), None),
        check_vma=False,
    )
```

profile of v0, /device:TPU:2, one launch (start us, length us, event | category | flops | bytes accessed | tf_op | source)
XLA Modules:
  0.0 386.3 jit_solution(990509101849732464)
XLA Ops:
  1.6 8.0 %all-to-all-start.1 = ((bf16[128,16,16]{0,2,1:T(8,128)(2,1)}), bf16[128,16,16]{0,2,1:T(8,128)(2,1)S(1)}, u32[]{:S(2)}, u32[]{:S(2)}) async-start(bf16[128,16,16]{0,2,1:T(8,128)(2,1)} %bitcast.7), calls=%async_computation.1 | async-start | bytes 131072 | tf_op jit(solution)/shard_map/all_to_all | solution.py:92
  12.4 4.9 %all-to-all-done.1 = bf16[128,16,16]{0,2,1:T(8,128)(2,1)S(1)} async-done(((bf16[128,16,16]{0,2,1:T(8,128)(2,1)}), bf16[128,16,16]{0,2,1:T(8,128)(2,1)S(1)}, u32[]{:S(2)}, u32[]{:S(2)}) %all-to-all-start.1) | async-done | bytes 65568 | tf_op jit(solution)/shard_map/all_to_all | solution.py:92
  18.8 3.7 all-to-all-start
  22.6 6.4 %copy.47 = bf16[128,16384]{0,1:T(8,128)(2,1)} copy(bf16[128,16384]{1,0:T(8,128)(2,1)} %param.11) | data formatting | bytes 8388608 | tf_op jit(solution)/shard_map/all_to_all | solution.py:91
  29.0 22.2 %all-to-all-done = bf16[128,16,512]{2,0,1:T(8,128)(2,1)S(1)} async-done(((bf16[128,16,512]{2,0,1:T(8,128)(2,1)}), bf16[128,16,512]{2,0,1:T(8,128)(2,1)S(1)}, u32[]{:S(2)}, u32[]{:S(2)}) %all-to-all-start) | async-done | bytes 2097184 | tf_op jit(solution)/shard_map/all_to_all | solution.py:93
  51.1 4.5 %all-to-all-start.2 = ((bf16[128,16,1024]{0,2,1:T(8,128)(2,1)}), bf16[128,16,1024]{0,2,1:T(8,128)(2,1)}, u32[]{:S(2)}, u32[]{:S(2)}) async-start(bf16[128,16,1024]{0,2,1:T(8,128)(2,1)} %bitcast.106), calls=%async_computation.2 | async-start | bytes 8388608 | tf_op jit(solution)/shard_map/all_to_all | solution.py:91
  57.5 1.6 fusion.25
  64.7 3.3 fusion.33
  72.5 1.7 fusion.32
  74.2 1.6 convert_element_type.32
  77.3 28.9 %all-to-all-done.2 = bf16[128,16,1024]{0,2,1:T(8,128)(2,1)} async-done(((bf16[128,16,1024]{0,2,1:T(8,128)(2,1)}), bf16[128,16,1024]{0,2,1:T(8,128)(2,1)}, u32[]{:S(2)}, u32[]{:S(2)}) %all-to-all-start.2) | async-done | bytes 4194336 | tf_op jit(solution)/shard_map/all_to_all | solution.py:91
  106.2 16.4 %fusion.1 = f32[16,16,256,64]{3,2,1,0:T(8,128)} fusion(bf16[16,128,16,64]{1,3,2,0:T(8,128)(2,1)} %bitcast.13, f32[16,128,16]{1,2,0:T(8,128)S(1)} %copy.37, f32[16,128,256]{2,1,0:T(8,128)} %convert_element_type.32), kind=kOutput, calls=%fused_computation.7 | convolution fusion | flops 1090519040 | bytes 23199744 | tf_op jit(solution)/shard_map/cjhn,cjhp->chnp/dot_general | solution.py:39
  122.6 57.8 %while.24 = (s32[]{:T(128)}, f32[16,256,64]{2,1,0:T(8,128)S(1)}, f32[16,16,256,64]{3,2,1,0:T(8,128)}, f32[16,16]{1,0:T(8,128)S(1)}, f32[16,16,256,64]{3,2,1,0:T(8,128)}, /*index=5*/s32[]{:T(128)}, s32[]{:T(128)}) while((s32[]{:T(128)}, f32[16,256,64]{2,1,0:T(8,128)S(1)}, f32[16,16,256,64]{3,2,1,0:T(8,128)}, ...), condition=%wide.region_2.3_spmd.clone, body=%wide.region_1.2_spmd.clone.sunk | while | flops 1048579 | bytes 6291756 | solution.py:63
  124.1 2.1 bitcast_add_fusion.2
  127.7 2.1 bitcast_add_fusion.2
  131.3 2.1 bitcast_add_fusion.2
  135.0 2.1 bitcast_add_fusion.2
  138.6 2.1 bitcast_add_fusion.2
  142.2 2.1 bitcast_add_fusion.2
  145.8 2.1 bitcast_add_fusion.2
  149.4 2.1 bitcast_add_fusion.2
  153.0 2.1 bitcast_add_fusion.2
  156.6 2.1 bitcast_add_fusion.2
  160.3 2.1 bitcast_add_fusion.2
  163.9 2.1 bitcast_add_fusion.2
  167.5 2.1 bitcast_add_fusion.2
  171.1 2.1 bitcast_add_fusion.2
  174.8 2.1 bitcast_add_fusion.2
  178.3 2.1 bitcast_add_fusion.2
  181.1 114.0 %while.23 = (s32[]{:T(128)}, f32[16,256,64]{1,2,0:T(8,128)S(1)}, f32[16]{0:T(128)S(1)}, f32[16,256,64]{1,2,0:T(8,128)S(1)}, s32[]{:T(128)}) while((s32[]{:T(128)}, f32[16,256,64]{1,2,0:T(8,128)S(1)}, f32[16]{0:T(128)S(1)}, f32[16,256,64]{1,2,0:T(8,128)S(1)}, s32[]{:T(128)}) %tuple.48), condition=%wide.region_5.6_spmd, body=%wide.region_4.5_spmd.sunk | while | flops 524290 | bytes 7340197 | solution.py:74
  181.3 1.9 collective-permute-start
  183.3 14.2 %collective-permute-done = f32[16,256,64]{1,2,0:T(8,128)S(1)} collective-permute-done((f32[16,256,64]{1,2,0:T(8,128)S(1)}, f32[16,256,64]{1,2,0:T(8,128)S(1)}, u32[]{:S(2)}, u32[]{:S(2)}) %collective-permute-start) | collective-permute-done | bytes 1048608 | tf_op jit(solution)/shard_map/while/body/eval_jaxpr/ppermute | solution.py:15
  197.6 1.9 collective-permute-start
  199.5 14.2 %collective-permute-done = f32[16,256,64]{1,2,0:T(8,128)S(1)} collective-permute-done((f32[16,256,64]{1,2,0:T(8,128)S(1)}, f32[16,256,64]{1,2,0:T(8,128)S(1)}, u32[]{:S(2)}, u32[]{:S(2)}) %collective-permute-start) | collective-permute-done | bytes 1048608 | tf_op jit(solution)/shard_map/while/body/eval_jaxpr/ppermute | solution.py:15
  213.9 1.9 collective-permute-start
  215.8 14.2 %collective-permute-done = f32[16,256,64]{1,2,0:T(8,128)S(1)} collective-permute-done((f32[16,256,64]{1,2,0:T(8,128)S(1)}, f32[16,256,64]{1,2,0:T(8,128)S(1)}, u32[]{:S(2)}, u32[]{:S(2)}) %collective-permute-start) | collective-permute-done | bytes 1048608 | tf_op jit(solution)/shard_map/while/body/eval_jaxpr/ppermute | solution.py:15
  230.2 1.9 collective-permute-start
  232.1 14.2 %collective-permute-done = f32[16,256,64]{1,2,0:T(8,128)S(1)} collective-permute-done((f32[16,256,64]{1,2,0:T(8,128)S(1)}, f32[16,256,64]{1,2,0:T(8,128)S(1)}, u32[]{:S(2)}, u32[]{:S(2)}) %collective-permute-start) | collective-permute-done | bytes 1048608 | tf_op jit(solution)/shard_map/while/body/eval_jaxpr/ppermute | solution.py:15
  246.5 1.9 collective-permute-start
  248.4 14.2 %collective-permute-done = f32[16,256,64]{1,2,0:T(8,128)S(1)} collective-permute-done((f32[16,256,64]{1,2,0:T(8,128)S(1)}, f32[16,256,64]{1,2,0:T(8,128)S(1)}, u32[]{:S(2)}, u32[]{:S(2)}) %collective-permute-start) | collective-permute-done | bytes 1048608 | tf_op jit(solution)/shard_map/while/body/eval_jaxpr/ppermute | solution.py:15
  262.8 1.9 collective-permute-start
  264.7 14.2 %collective-permute-done = f32[16,256,64]{1,2,0:T(8,128)S(1)} collective-permute-done((f32[16,256,64]{1,2,0:T(8,128)S(1)}, f32[16,256,64]{1,2,0:T(8,128)S(1)}, u32[]{:S(2)}, u32[]{:S(2)}) %collective-permute-start) | collective-permute-done | bytes 1048608 | tf_op jit(solution)/shard_map/while/body/eval_jaxpr/ppermute | solution.py:15
  279.1 1.9 collective-permute-start
  281.0 14.2 %collective-permute-done = f32[16,256,64]{1,2,0:T(8,128)S(1)} collective-permute-done((f32[16,256,64]{1,2,0:T(8,128)S(1)}, f32[16,256,64]{1,2,0:T(8,128)S(1)}, u32[]{:S(2)}, u32[]{:S(2)}) %collective-permute-start) | collective-permute-done | bytes 1048608 | tf_op jit(solution)/shard_map/while/body/eval_jaxpr/ppermute | solution.py:15
  295.8 16.5 %fusion.2 = f32[16,16,64,128]{3,2,1,0:T(8,128)} fusion(bf16[16,128,256,1]{2,1,3,0:T(8,128)(2,1)} %bitcast.109, f32[16,16,256,64]{3,2,1,0:T(8,128)} %get-tuple-element.55, f32[16,256,64]{2,1,0:T(8,128)S(1)} %copy.40, f32[16,16]{1,0:T(8,128)S(1)} %get-tuple-element.117), kind=kOutput, calls=%fused_computation.8 | convolution fusion | flops 1086324736 | bytes 27264000 | tf_op jit(solution)/shard_map/cign,cgknp->cigkp/dot_general | solution.py:48
  312.4 11.9 %fusion.10 = bf16[16,128,16,64]{1,3,2,0:T(8,128)(2,1)S(1)} fusion(f32[16,16,64,128]{3,2,1,0:T(8,128)} %fusion.2, bf16[16,128,16,64]{1,3,2,0:T(8,128)(2,1)} %bitcast.13, f32[16]{0:T(128)S(1)} %copy-done.8, f32[16,128,16]{1,2,0:T(8,128)S(1)} %copy.42, f32[16,16,128]{2,1,0:T(8,128)S(1)} %copy.35, f32[16,16,128]{2,1,0:T(8,128)S(1)} %copy.33, ...), kind=kOutput, calls=%fused_computation.18 | convolution fusion | flops 570425344 | bytes 18235456 | tf_op jit(solution)/shard_map/chij,cjhp->cihp/dot_general | solution.py:35
  324.3 55.7 %all_to_all.67 = bf16[16,128,1024]{1,2,0:T(8,128)(2,1)} all-to-all(bf16[16,128,1024]{1,2,0:T(8,128)(2,1)S(1)} %bitcast.115), channel_id=1, replica_groups=mesh['ctx'=16,'seq'=8] {'ctx'}, dimensions={0} | all-to-all | bytes 8388608 | tf_op jit(solution)/shard_map/all_to_all | solution.py:113
  380.0 6.4 %copy.48 = bf16[128,16384]{1,0:T(8,128)(2,1)} copy(bf16[128,16384]{0,1:T(8,128)(2,1)} %bitcast.107) | data formatting | bytes 8388608 | tf_op jit(solution)/shard_map/all_to_all | solution.py:113
  (84 shorter events, 45.5 us)
Async XLA Ops:
  1.6 15.7 %all-to-all-start.1 = ((bf16[128,16,16]{0,2,1:T(8,128)(2,1)}), bf16[128,16,16]{0,2,1:T(8,128)(2,1)S(1)}, u32[]{:S(2)}, u32[]{:S(2)}) async-start(bf16[128,16,16]{0,2,1:T(8,128)(2,1)} %bitcast.7), calls=%async_computation.1 | async-start | bytes 131072 | tf_op jit(solution)/shard_map/all_to_all | solution.py:92
  18.8 32.3 %all-to-all-start = ((bf16[128,16,512]{2,0,1:T(8,128)(2,1)}), bf16[128,16,512]{2,0,1:T(8,128)(2,1)S(1)}, u32[]{:S(2)}, u32[]{:S(2)}) async-start(bf16[128,16,512]{2,0,1:T(8,128)(2,1)} %bitcast.114), calls=%async_computation | async-start | bytes 4194304 | tf_op jit(solution)/shard_map/all_to_all | solution.py:93
  22.6 33.2 %copy-start.6 = (f32[256]{0:T(256)S(1)}, f32[256]{0:T(256)}, u32[]{:S(2)}) copy-start(f32[256]{0:T(256)} %param.15) | copy-start | bytes 3076
  22.6 33.2 %copy-start.7 = (f32[256]{0:T(256)S(1)}, f32[256]{0:T(256)}, u32[]{:S(2)}) copy-start(f32[256]{0:T(256)} %param.17) | copy-start | bytes 3076
  22.6 33.8 %copy-start.5 = (f32[256]{0:T(256)S(1)}, f32[256]{0:T(256)}, u32[]{:S(2)}) copy-start(f32[256]{0:T(256)} %param.16) | copy-start | bytes 3076
  51.1 4.6 %copy-start.1 = (bf16[128,16,512]{2,0,1:T(8,128)(2,1)}, bf16[128,16,512]{2,0,1:T(8,128)(2,1)S(1)}, u32[]{:S(2)}) copy-start(bf16[128,16,512]{2,0,1:T(8,128)(2,1)S(1)} %all-to-all-done) | copy-start | bytes 6291460
  51.1 55.1 %all-to-all-start.2 = ((bf16[128,16,1024]{0,2,1:T(8,128)(2,1)}), bf16[128,16,1024]{0,2,1:T(8,128)(2,1)}, u32[]{:S(2)}, u32[]{:S(2)}) async-start(bf16[128,16,1024]{0,2,1:T(8,128)(2,1)} %bitcast.106), calls=%async_computation.2 | async-start | bytes 8388608 | tf_op jit(solution)/shard_map/all_to_all | solution.py:91
  74.2 1.6 copy-start
  122.6 58.5 %copy-start.4 = (f32[16]{0:T(128)S(1)}, f32[16]{0:T(128)}, u32[]{:S(2)}) copy-start(f32[16]{0:T(128)} %fusion.28) | copy-start | bytes 196
  181.3 16.1 %collective-permute-start = (f32[16,256,64]{1,2,0:T(8,128)S(1)}, f32[16,256,64]{1,2,0:T(8,128)S(1)}, u32[]{:S(2)}, u32[]{:S(2)}) collective-permute-start(f32[16,256,64]{1,2,0:T(8,128)S(1)} %multiply_add_fusion.2), channel_id=1, source_target_pairs={{0,1},{1,2},{2,3},{3,4},{4,5},{5,6},{6,7},{8,9},{9,10},{10,11},{11... | collective-permute-start | bytes 3145736 | tf_op jit(solution)/shard_map/while/body/eval_jaxpr/ppermute | solution.py:15
  197.6 16.1 %collective-permute-start = (f32[16,256,64]{1,2,0:T(8,128)S(1)}, f32[16,256,64]{1,2,0:T(8,128)S(1)}, u32[]{:S(2)}, u32[]{:S(2)}) collective-permute-start(f32[16,256,64]{1,2,0:T(8,128)S(1)} %multiply_add_fusion.2), channel_id=1, source_target_pairs={{0,1},{1,2},{2,3},{3,4},{4,5},{5,6},{6,7},{8,9},{9,10},{10,11},{11... | collective-permute-start | bytes 3145736 | tf_op jit(solution)/shard_map/while/body/eval_jaxpr/ppermute | solution.py:15
  213.9 16.1 %collective-permute-start = (f32[16,256,64]{1,2,0:T(8,128)S(1)}, f32[16,256,64]{1,2,0:T(8,128)S(1)}, u32[]{:S(2)}, u32[]{:S(2)}) collective-permute-start(f32[16,256,64]{1,2,0:T(8,128)S(1)} %multiply_add_fusion.2), channel_id=1, source_target_pairs={{0,1},{1,2},{2,3},{3,4},{4,5},{5,6},{6,7},{8,9},{9,10},{10,11},{11... | collective-permute-start | bytes 3145736 | tf_op jit(solution)/shard_map/while/body/eval_jaxpr/ppermute | solution.py:15
  230.2 16.1 %collective-permute-start = (f32[16,256,64]{1,2,0:T(8,128)S(1)}, f32[16,256,64]{1,2,0:T(8,128)S(1)}, u32[]{:S(2)}, u32[]{:S(2)}) collective-permute-start(f32[16,256,64]{1,2,0:T(8,128)S(1)} %multiply_add_fusion.2), channel_id=1, source_target_pairs={{0,1},{1,2},{2,3},{3,4},{4,5},{5,6},{6,7},{8,9},{9,10},{10,11},{11... | collective-permute-start | bytes 3145736 | tf_op jit(solution)/shard_map/while/body/eval_jaxpr/ppermute | solution.py:15
  246.5 16.1 %collective-permute-start = (f32[16,256,64]{1,2,0:T(8,128)S(1)}, f32[16,256,64]{1,2,0:T(8,128)S(1)}, u32[]{:S(2)}, u32[]{:S(2)}) collective-permute-start(f32[16,256,64]{1,2,0:T(8,128)S(1)} %multiply_add_fusion.2), channel_id=1, source_target_pairs={{0,1},{1,2},{2,3},{3,4},{4,5},{5,6},{6,7},{8,9},{9,10},{10,11},{11... | collective-permute-start | bytes 3145736 | tf_op jit(solution)/shard_map/while/body/eval_jaxpr/ppermute | solution.py:15
  262.8 16.1 %collective-permute-start = (f32[16,256,64]{1,2,0:T(8,128)S(1)}, f32[16,256,64]{1,2,0:T(8,128)S(1)}, u32[]{:S(2)}, u32[]{:S(2)}) collective-permute-start(f32[16,256,64]{1,2,0:T(8,128)S(1)} %multiply_add_fusion.2), channel_id=1, source_target_pairs={{0,1},{1,2},{2,3},{3,4},{4,5},{5,6},{6,7},{8,9},{9,10},{10,11},{11... | collective-permute-start | bytes 3145736 | tf_op jit(solution)/shard_map/while/body/eval_jaxpr/ppermute | solution.py:15
  279.1 16.1 %collective-permute-start = (f32[16,256,64]{1,2,0:T(8,128)S(1)}, f32[16,256,64]{1,2,0:T(8,128)S(1)}, u32[]{:S(2)}, u32[]{:S(2)}) collective-permute-start(f32[16,256,64]{1,2,0:T(8,128)S(1)} %multiply_add_fusion.2), channel_id=1, source_target_pairs={{0,1},{1,2},{2,3},{3,4},{4,5},{5,6},{6,7},{8,9},{9,10},{10,11},{11... | collective-permute-start | bytes 3145736 | tf_op jit(solution)/shard_map/while/body/eval_jaxpr/ppermute | solution.py:15
  295.8 16.6 %copy-start.2 = (f32[16,128,128]{2,1,0:T(8,128)S(1)}, f32[16,128,128]{2,1,0:T(8,128)}, u32[]{:S(2)}) copy-start(f32[16,128,128]{2,1,0:T(8,128)} %fusion.34) | copy-start | bytes 3145732
  295.8 16.6 %copy-start.3 = (pred[128,128]{1,0:T(8,128)(4,1)S(1)}, pred[128,128]{1,0:T(8,128)(4,1)}, u32[]{:S(2)}) copy-start(pred[128,128]{1,0:T(8,128)(4,1)} %iota_compare_fusion) | copy-start | bytes 49156
  295.8 16.6 %copy-start.8 = (f32[16]{0:T(128)S(1)}, f32[16]{0:T(128)}, u32[]{:S(2)}) copy-start(f32[16]{0:T(128)} %dynamic_slice.19) | copy-start | bytes 196
where the time goes:
time: 388 us; the launch traced here: 386 us
  waiting for transfers between devices  155 us (40%)
  other arithmetic  68 us (18%)
  blocking collectives  55.7 us (14%)
  matrix products  46.3 us (12%)
  local copies, waits for them, and re-layouts  30.4 us (8%)
  starting transfers between devices  29.8 us (8%)
    ppermute x7, waiting for transfers between devices, from_behind(): lax.ppermute(value, axis, [(source, source + steps) for source in range(l...  99.3 us
    all_to_all x1, blocking collectives, body(): lax.all_to_all(result.reshape(block, local * P_SIZE), 'ctx', split_axis=0...  55.7 us
    add x16, other arithmetic, advance(): return (factor[:, None, None] * carry + piece, carry)  33.3 us
    all_to_all x1, waiting for transfers between devices, body(): lax.all_to_all(mixer_input, 'ctx', split_axis=1, concat_axis=0, tiled=True)  28.9 us
    dynamic_update_slice x16, other arithmetic, apply_segmented_scan(): lax.scan(advance, jnp.zeros_like(states[0]), (jnp.exp(logs), states))  23.8 us
    all_to_all x1, waiting for transfers between devices, body(): lax.all_to_all(paired, 'ctx', split_axis=1, concat_axis=0, tiled=True)  22.2 us
    dot_general x1, matrix products, off_part(): jnp.einsum('cign,cgknp->cigkp', c_span, entry_bf.reshape(count, groups, s...  16.5 us
    dot_general x1, matrix products, span_parts(): jnp.einsum('cjhn,cjhp->chnp', weighted, inputs_x, preferred_element_type=...  16.4 us
  transfers between devices with their start and end apart: 10, of which 10 were waited for; matrix products, arithmetic and copies ran while one was open for 8% of the time, Pallas kernels for 0%

commit v1 on v0

v1 whole, which is shorter than its diff:
```python
import functools

import jax
import jax.numpy as jnp
from jax import lax
from jax.experimental import pallas as pl
from jax.experimental.pallas import tpu as pltpu
from jax.sharding import PartitionSpec as P

P_SIZE = 64
N = 256
CHUNKS = 4


def scan_kernel(
    nc,
    ns,
    groups,
    x_hbm,
    step_ref,
    b_hbm,
    c_hbm,
    bias_ref,
    dlog_ref,
    gain_ref,
    o_hbm,
    xv,
    bv,
    cv,
    xw,
    spread,
    w2,
    ec2,
    dsend,
    rb,
    rc,
    rx,
    rd,
    states,
    whole,
    cin,
    cout,
    offs,
    offr,
    part,
    load_sem,
    sb_sem,
    sc_sem,
    sd_sem,
    sx_sem,
    so_sem,
    sch_sem,
    rb_sem,
    rc_sem,
    rd_sem,
    rx_sem,
    ro_sem,
    rch_sem,
    out_sem,
):
    f32, bf16 = jnp.float32, jnp.bfloat16
    me = lax.axis_index("ctx")
    sq = lax.axis_index("seq")
    tok, width = xv.shape
    heads = step_ref.shape[1]
    own = width // nc
    cw = own // CHUNKS
    share = heads // groups
    gw = share * P_SIZE
    rep = nc // groups

    loads = (
        pltpu.make_async_copy(x_hbm, xv, load_sem.at[0]),
        pltpu.make_async_copy(b_hbm, bv, load_sem.at[1]),
        pltpu.make_async_copy(c_hbm, cv, load_sem.at[2]),
    )
    for load in loads:
        load.start()

    barrier = pltpu.get_barrier_semaphore()

    def greet(k, carry):
        pl.semaphore_signal(barrier, inc=1, device_id={"ctx": lax.rem(me + k, nc)})
        return carry

    lax.fori_loop(1, nc, greet, 0)

    @pl.when(sq > 0)
    def _():
        pl.semaphore_signal(barrier, inc=1, device_id={"seq": sq - 1})

    @pl.when(sq < ns - 1)
    def _():
        pl.semaphore_signal(barrier, inc=1, device_id={"seq": sq + 1})

    links = (sq > 0).astype(jnp.int32) + (sq < ns - 1).astype(jnp.int32)
    pl.semaphore_wait(barrier, nc - 1 + links)

    def columns(start, size):
        return pl.ds(pl.multiple_of(start, 128), size)

    def send_group(src, dst, send_sem, recv_sem):
        def one(k, carry):
            peer = lax.rem(me + k, nc)
            pltpu.make_async_remote_copy(
                src_ref=src.at[:, columns(lax.div(peer, rep) * N, N)],
                dst_ref=dst.at[me],
                send_sem=send_sem,
                recv_sem=recv_sem,
                device_id={"ctx": peer},
            ).start()
            return carry

        lax.fori_loop(1, nc, one, 0)

    def send_x(c):
        def one(k, carry):
            peer = lax.rem(me + k, nc)
            pltpu.make_async_remote_copy(
                src_ref=xw.at[:, columns(peer * own + c * cw, cw)],
                dst_ref=rx.at[c, me],
                send_sem=sx_sem.at[c],
                recv_sem=rx_sem.at[c],
                device_id={"ctx": peer},
            ).start()
            return carry

        lax.fori_loop(1, nc, one, 0)
        pltpu.make_async_copy(
            xw.at[:, columns(me * own + c * cw, cw)], rx.at[c, me], rx_sem.at[c]
        ).start()

    send_group(b_hbm, rb, sb_sem, rb_sem)

    v = step_ref[...].astype(f32) + bias_ref[...]
    dt = jnp.maximum(v, 0.0) + jnp.log1p(jnp.exp(-jnp.abs(v)))
    rate = dt * (-jnp.exp(dlog_ref[...]))
    rows = lax.broadcasted_iota(jnp.int32, (tok, tok), 0)
    cols = lax.broadcasted_iota(jnp.int32, (tok, tok), 1)
    tri = (rows >= cols).astype(f32)
    cum = jnp.dot(tri, rate, precision=lax.Precision.HIGHEST, preferred_element_type=f32)
    w = dt * jnp.exp(-cum)
    ec = jnp.exp(cum)
    w_hi = w.astype(bf16)
    w_lo = (w - w_hi.astype(f32)).astype(bf16)
    e_hi = ec.astype(bf16)
    e_lo = (ec - e_hi.astype(f32)).astype(bf16)
    gain = jnp.broadcast_to(gain_ref[...], (16, heads))
    g_hi = gain.astype(bf16)
    g_lo = (gain - g_hi.astype(f32)).astype(bf16)
    for g in range(groups):
        part_of = slice(g * share, (g + 1) * share)
        w2[g, :, :share] = w_hi[:, part_of]
        w2[g, :, share:] = w_lo[:, part_of]
        ec2[g, :tok, :share] = e_hi[:, part_of]
        ec2[g, :tok, share:] = e_lo[:, part_of]
        ec2[g, tok:, :share] = g_hi[:, part_of]
        ec2[g, tok:, share:] = g_lo[:, part_of]
    slot_of = lax.broadcasted_iota(jnp.int32, (2 * share, gw), 0)
    lane_of = lax.broadcasted_iota(jnp.int32, (2 * share, gw), 1)
    spread[...] = jnp.where(lax.rem(slot_of, share) == lax.div(lane_of, P_SIZE), 1.0, 0.0).astype(bf16)

    ends = lax.dot_general(
        rate,
        jnp.ones((tok, 128), f32),
        (((0,), (0,)), ((), ())),
        precision=lax.Precision.HIGHEST,
        preferred_element_type=f32,
    )
    head_of = lax.broadcasted_iota(jnp.int32, (heads, 128), 0)
    half_of = lax.div(lax.broadcasted_iota(jnp.int32, (heads, 128), 1), P_SIZE)
    halves = jnp.where(lax.rem(head_of, 2) == half_of, jnp.exp(ends), 0.0)
    pair_row = lax.broadcasted_iota(jnp.int32, (heads // 2, heads), 0)
    pair_col = lax.div(lax.broadcasted_iota(jnp.int32, (heads // 2, heads), 1), 2)
    pick = (pair_row == pair_col).astype(f32)
    tiles = jnp.dot(pick, halves, precision=lax.Precision.HIGHEST, preferred_element_type=f32)
    dsend[...] = tiles.reshape(nc, own // 128, 128)

    loads[0].wait()

    def weigh(g, carry):
        at = columns(g * gw, gw)
        spread_w = jnp.dot(w2[g], spread[...], preferred_element_type=f32)
        xw[:, at] = (xv[:, at].astype(f32) * spread_w).astype(bf16)
        return carry

    lax.fori_loop(0, groups, weigh, 0)

    def send_d(k, carry):
        peer = lax.rem(me + k, nc)
        pltpu.make_async_remote_copy(
            src_ref=dsend.at[peer],
            dst_ref=rd.at[me],
            send_sem=sd_sem,
            recv_sem=rd_sem,
            device_id={"ctx": peer},
        ).start()
        return carry

    lax.fori_loop(1, nc, send_d, 0)
    pltpu.make_async_copy(dsend.at[me], rd.at[me], rd_sem).start()
    send_x(0)
    send_x(1)
    send_group(c_hbm, rc, sc_sem, rc_sem)
    for c in range(2, CHUNKS):
        send_x(c)

    loads[1].wait()
    loads[2].wait()
    mine = columns(lax.div(me, rep) * N, N)
    pltpu.make_async_copy(bv.at[:, mine], rb.at[me], rb_sem).start()
    pltpu.make_async_copy(cv.at[:, mine], rc.at[me], rc_sem).start()

    def local_part(g):
        at = columns(g * gw, gw)
        state_at = columns(g * N, N)
        inner = lax.dot_general(
            cv[:, state_at], bv[:, state_at], (((1,), (1,)), ((), ())), preferred_element_type=f32
        )
        inner = jnp.where(rows >= cols, inner, 0.0).astype(bf16)
        diag = jnp.dot(inner, xw[:, at], preferred_element_type=f32)
        scale = jnp.dot(ec2[g], spread[...], preferred_element_type=f32)
        part[:, at] = scale[:tok] * diag + scale[tok : tok + 1] * xv[:, at].astype(f32)

    def local_range(low, high):
        def one(g, carry):
            local_part(g)
            return carry

        lax.fori_loop(low, high, one, 0)

    def decay_row(c, s):
        per = cw // 128
        tile = rd[s]
        return jnp.concatenate([tile[c * per + r : c * per + r + 1] for r in range(per)], axis=1)

    def gather_states(c):
        pltpu.make_async_copy(rx.at[c], rx.at[c], rx_sem.at[c]).wait()
        slot = c % 2
        cout[c] = jnp.zeros(cout.shape[1:], f32)

        def one(s, total):
            piece = lax.dot_general(
                rb[s], rx[c, s], (((0,), (0,)), ((), ())), preferred_element_type=f32
            )
            factor = decay_row(c, s)
            states[slot, s] = piece
            cout[c] = factor * (cout[c] + piece)
            return total * factor

        whole[c] = lax.fori_loop(0, nc, one, jnp.ones((1, cw), f32))

    def pass_on(c):
        return pltpu.make_async_remote_copy(
            src_ref=cout.at[c],
            dst_ref=cin.at[c],
            send_sem=sch_sem.at[c],
            recv_sem=rch_sem.at[c],
            device_id={"seq": lax.rem(sq + 1, ns)},
        )

    def chain(c):
        @pl.when(sq > 0)
        def _():
            pass_on(c).wait_recv()

        @pl.when(sq == 0)
        def _():
            cin[c] = jnp.zeros(cin.shape[1:], f32)

        @pl.when(sq < ns - 1)
        def _():
            cout[c] = whole[c] * cin[c] + cout[c]
            pass_on(c).start()

    def read_states(c):
        slot = c % 2

        def one(s, carry):
            entry = cin[c]
            offs[c, s] = jnp.dot(rc[s], entry.astype(bf16), preferred_element_type=f32).astype(bf16)
            cin[c] = decay_row(c, s) * (entry + states[slot, s])
            return carry

        lax.fori_loop(0, nc, one, 0)
        at = columns(me * own + c * cw, cw)

        def send(k, carry):
            peer = lax.rem(me + k, nc)
            pltpu.make_async_remote_copy(
                src_ref=offs.at[c, peer],
                dst_ref=offr.at[:, at],
                send_sem=so_sem.at[c],
                recv_sem=ro_sem.at[c],
                device_id={"ctx": peer},
            ).start()
            return carry

        lax.fori_loop(1, nc, send, 0)
        pltpu.make_async_copy(offs.at[c, me], offr.at[:, at], ro_sem.at[c]).start()

    def combine(c):
        pltpu.make_async_copy(rx.at[c], rx.at[c], ro_sem.at[c]).wait()

        def one(o, carry):
            at = columns(o * own + c * cw, cw)
            within = columns(lax.rem(o, rep) * own + c * cw, cw)
            g = lax.div(o, rep)
            scale = jnp.dot(ec2[g, :tok, :], spread[:, within], preferred_element_type=f32)
            offr[:, at] = (part[:, at] + scale * offr[:, at].astype(f32)).astype(bf16)
            pltpu.make_async_copy(offr.at[:, at], o_hbm.at[:, at], out_sem.at[c]).start()
            return carry

        lax.fori_loop(0, nc, one, 0)

    quarter = groups // 4
    pltpu.make_async_copy(rb, rb, rb_sem).wait()
    pltpu.make_async_copy(rd, rd, rd_sem).wait()
    local_range(0, quarter)
    gather_states(0)
    local_range(quarter, 2 * quarter)
    gather_states(1)
    chain(0)
    pltpu.make_async_copy(rc, rc, rc_sem).wait()
    read_states(0)
    local_range(2 * quarter, 3 * quarter)
    gather_states(2)
    chain(1)
    read_states(1)
    local_range(3 * quarter, groups)
    gather_states(3)
    chain(2)
    read_states(2)
    chain(3)
    read_states(3)
    for c in range(CHUNKS):
        combine(c)

    for c in range(CHUNKS):
        pltpu.make_async_copy(rx.at[c, 1:], rx.at[c, 1:], sx_sem.at[c]).wait()
        pltpu.make_async_copy(offs.at[c, 1:], offs.at[c, 1:], so_sem.at[c]).wait()

        @pl.when(sq < ns - 1)
        def _():
            pass_on(c).wait_send()

    pltpu.make_async_copy(rb.at[1:], rb.at[1:], sb_sem).wait()
    pltpu.make_async_copy(rc.at[1:], rc.at[1:], sc_sem).wait()
    pltpu.make_async_copy(rd.at[1:], rd.at[1:], sd_sem).wait()
    for c in range(CHUNKS):
        pltpu.make_async_copy(rx.at[c], rx.at[c], out_sem.at[c]).wait()


def body(mixer_input, step_raw, b_proj, c_proj, step_bias, decay_log, skip_gain):
    nc, ns = lax.axis_size("ctx"), lax.axis_size("seq")
    tok, width = mixer_input.shape
    heads = step_raw.shape[1]
    groups = b_proj.shape[1] // N
    share = heads // groups
    own = width // nc
    cw = own // CHUNKS
    f32, bf16 = jnp.float32, jnp.bfloat16
    any_spec = pl.BlockSpec(memory_space=pl.ANY)
    vmem_spec = pl.BlockSpec(memory_space=pltpu.VMEM)
    dma = pltpu.SemaphoreType.DMA
    return pl.pallas_call(
        functools.partial(scan_kernel, nc, ns, groups),
        out_shape=jax.ShapeDtypeStruct((tok, width), bf16),
        in_specs=[any_spec, vmem_spec, any_spec, any_spec, vmem_spec, vmem_spec, vmem_spec],
        out_specs=any_spec,
        scratch_shapes=[
            pltpu.VMEM((tok, width), bf16),
            pltpu.VMEM((tok, groups * N), bf16),
            pltpu.VMEM((tok, groups * N), bf16),
            pltpu.VMEM((tok, width), bf16),
            pltpu.VMEM((2 * share, share * P_SIZE), bf16),
            pltpu.VMEM((groups, tok, 2 * share), bf16),
            pltpu.VMEM((groups, tok + 16, 2 * share), bf16),
            pltpu.VMEM((nc, own // 128, 128), f32),
            pltpu.VMEM((nc, tok, N), bf16),
            pltpu.VMEM((nc, tok, N), bf16),
            pltpu.VMEM((CHUNKS, nc, tok, cw), bf16),
            pltpu.VMEM((nc, own // 128, 128), f32),
            pltpu.VMEM((2, nc, N, cw), f32),
            pltpu.VMEM((CHUNKS, 1, cw), f32),
            pltpu.VMEM((CHUNKS, N, cw), f32),
            pltpu.VMEM((CHUNKS, N, cw), f32),
            pltpu.VMEM((CHUNKS, nc, tok, cw), bf16),
            pltpu.VMEM((tok, width), bf16),
            pltpu.VMEM((tok, width), f32),
            dma((3,)),
            dma,
            dma,
            dma,
            dma((CHUNKS,)),
            dma((CHUNKS,)),
            dma((CHUNKS,)),
            dma,
            dma,
            dma,
            dma((CHUNKS,)),
            dma((CHUNKS,)),
            dma((CHUNKS,)),
            dma((CHUNKS,)),
        ],
        compiler_params=pltpu.CompilerParams(
            collective_id=0, has_side_effects=True, vmem_limit_bytes=62 * 1024 * 1024
        ),
    )(
        mixer_input,
        step_raw,
        b_proj,
        c_proj,
        step_bias.reshape(1, heads),
        decay_log.reshape(1, heads),
        skip_gain.reshape(1, heads),
    )


def solution(mesh):
    return jax.shard_map(
        body,
        mesh=mesh,
        in_specs=(
            P(("seq", "ctx"), None),
            P(("seq", "ctx"), None),
            P(("seq", "ctx"), None),
            P(("seq", "ctx"), None),
            P(),
            P(),
            P(),
        ),
        out_specs=P(("seq", "ctx"), None),
        check_vma=False,
    )
```

time: 388 us -> 191 us (0.49)
  the two profiles are of different devices: /device:TPU:2 before, /device:TPU:119 now
where the time goes in v1:
time: 191 us
  Pallas kernels  187 us (98%)
  local copies, waits for them, and re-layouts  4.57 us (2%)
    pallas_call x1, Pallas kernels, body(): pl.pallas_call(functools.partial(scan_kernel, nc, ns, groups), out_shape=...  187 us
    unnamed x1, local copies, waits for them, and re-layouts  4.57 us

profile of v1, /device:TPU:119, one launch (start us, length us, event | category | flops | bytes accessed | tf_op | source)
XLA Modules:
  0.0 191.1 jit_solution(17413748299671527808)
XLA Ops:
  0.0 186.5 %shard_map.73 = bf16[128,16384]{1,0:T(8,128)(2,1)} custom-call(bf16[128,16384]{1,0:T(8,128)(2,1)} %x_hbm.1, bf16[128,256]{1,0:T(8,128)(2,1)} %step_ref.1, bf16[128,2048]{1,0:T(8,128)(2,1)} %b_hbm.1, bf16[128,2048]{1,0:T(8,128)(2,1)} %c_hbm.1, f32[1,256]{1,0:T(1,128)} %bitcast.3, f32[1,256]{1,0:T(1,128)} %bitcast.4, f32[1,256]{1,0:T(1,128)} %bitcast.5), custom_call_target="tpu_custom_call" | custom-call | tf_op jit(solution)/shard_map/pallas_call | solution.py:366
  186.5 4.6 %copy.9 = bf16[128,16384]{1,0:T(8,128)(2,1)} copy(bf16[128,16384]{1,0:T(8,128)(2,1)} %shard_map.73) | data formatting | bytes 8388608

commit v2 on v1

--- a/solution.py
+++ b/solution.py
@@ -69,6 +69,13 @@
     gw = share * P_SIZE
     rep = nc // groups
 
+    side = 4 if nc % 4 == 0 else 1
+    rank = nc // side
+    row, col = lax.div(me, side), lax.rem(me, side)
+
+    def partner(k):
+        return lax.rem(row + lax.div(k, side), rank) * side + lax.rem(col + lax.rem(k, side), side)
+
     loads = (
         pltpu.make_async_copy(x_hbm, xv, load_sem.at[0]),
         pltpu.make_async_copy(b_hbm, bv, load_sem.at[1]),
@@ -80,7 +87,7 @@
     barrier = pltpu.get_barrier_semaphore()
 
     def greet(k, carry):
-        pl.semaphore_signal(barrier, inc=1, device_id={"ctx": lax.rem(me + k, nc)})
+        pl.semaphore_signal(barrier, inc=1, device_id={"ctx": partner(k)})
         return carry
 
     lax.fori_loop(1, nc, greet, 0)
@@ -101,7 +108,7 @@
 
     def send_group(src, dst, send_sem, recv_sem):
         def one(k, carry):
-            peer = lax.rem(me + k, nc)
+            peer = partner(k)
             pltpu.make_async_remote_copy(
                 src_ref=src.at[:, columns(lax.div(peer, rep) * N, N)],
                 dst_ref=dst.at[me],
@@ -115,7 +122,7 @@
 
     def send_x(c):
         def one(k, carry):
-            peer = lax.rem(me + k, nc)
+            peer = partner(k)
             pltpu.make_async_remote_copy(
                 src_ref=xw.at[:, columns(peer * own + c * cw, cw)],
                 dst_ref=rx.at[c, me],
@@ -187,7 +194,7 @@
     lax.fori_loop(0, groups, weigh, 0)
 
     def send_d(k, carry):
-        peer = lax.rem(me + k, nc)
+        peer = partner(k)
         pltpu.make_async_remote_copy(
             src_ref=dsend.at[peer],
             dst_ref=rd.at[me],
@@ -286,7 +293,7 @@
         at = columns(me * own + c * cw, cw)
 
         def send(k, carry):
-            peer = lax.rem(me + k, nc)
+            peer = partner(k)
             pltpu.make_async_remote_copy(
                 src_ref=offs.at[c, peer],
                 dst_ref=offr.at[:, at],

time: 191 us -> 147 us (0.77)
  Pallas kernels: 187 us -> 142 us
    pallas_call x1, Pallas kernels: 187 us -> 142 us  [body(): pl.pallas_call(functools.partial(scan_kernel, nc, ns, groups), out_shape=...]
where the time goes in v2:
time: 147 us
  Pallas kernels  142 us (97%)
  local copies, waits for them, and re-layouts  4.57 us (3%)
    pallas_call x1, Pallas kernels, body(): pl.pallas_call(functools.partial(scan_kernel, nc, ns, groups), out_shape=...  142 us
    unnamed x1, local copies, waits for them, and re-layouts  4.57 us

profile of v2, /device:TPU:119, one launch (start us, length us, event | category | flops | bytes accessed | tf_op | source)
XLA Modules:
  0.0 146.6 jit_solution(3627428877952711033)
XLA Ops:
  0.0 142.0 %shard_map.73 = bf16[128,16384]{1,0:T(8,128)(2,1)} custom-call(bf16[128,16384]{1,0:T(8,128)(2,1)} %x_hbm.1, bf16[128,256]{1,0:T(8,128)(2,1)} %step_ref.1, bf16[128,2048]{1,0:T(8,128)(2,1)} %b_hbm.1, bf16[128,2048]{1,0:T(8,128)(2,1)} %c_hbm.1, f32[1,256]{1,0:T(1,128)} %bitcast.3, f32[1,256]{1,0:T(1,128)} %bitcast.4, f32[1,256]{1,0:T(1,128)} %bitcast.5), custom_call_target="tpu_custom_call" | custom-call | tf_op jit(solution)/shard_map/pallas_call | solution.py:373
  142.0 4.6 %copy.9 = bf16[128,16384]{1,0:T(8,128)(2,1)} copy(bf16[128,16384]{1,0:T(8,128)(2,1)} %shard_map.73) | data formatting | bytes 8388608

commit v3 on v2

v3 whole, which is shorter than its diff:
```python
import functools

import jax
import jax.numpy as jnp
from jax import lax
from jax.experimental import pallas as pl
from jax.experimental.pallas import tpu as pltpu
from jax.sharding import PartitionSpec as P

P_SIZE = 64
N = 256
CHUNKS = 8
SLOTS = 4


def scan_kernel(
    nc,
    ns,
    groups,
    x_hbm,
    step_ref,
    b_hbm,
    c_hbm,
    bias_ref,
    dlog_ref,
    gain_ref,
    o_ref,
    xv,
    bv,
    cv,
    xw,
    spread,
    w2,
    ec2,
    dsend,
    rb,
    rc,
    rx,
    rd,
    states,
    total,
    whole,
    entry,
    pre,
    pre_d,
    run,
    run_d,
    head,
    nexthead,
    offs,
    offr,
    part,
    load_sem,
    sb_sem,
    sc_sem,
    sd_sem,
    sx_sem,
    so_sem,
    sr_sem,
    srd_sem,
    sh_sem,
    rb_sem,
    rc_sem,
    rd_sem,
    rx_sem,
    ro_sem,
    rr_sem,
    rrd_sem,
    rh_sem,
):
    f32, bf16 = jnp.float32, jnp.bfloat16
    me = lax.axis_index("ctx")
    sq = lax.axis_index("seq")
    tok, width = xv.shape
    heads = step_ref.shape[1]
    cw = width // groups // CHUNKS
    share = heads // groups
    gw = share * P_SIZE
    side = groups // 2
    half, span = lax.div(me, groups), lax.rem(me, groups)
    row, col = lax.div(span, side), lax.rem(span, side)
    flip = half * side
    mine = lax.rem(span + flip, groups)
    across = (1 - half) * groups + lax.rem(span + side, groups)
    role = lax.rem(sq, 2) * 2 + half
    block = lax.div(sq, 2)
    blocks = ns // 2
    inner_x = block < blocks - 1

    def partner(k):
        return lax.rem(row + lax.div(k, side), 2) * side + lax.rem(col + lax.rem(k, side), side)

    def source(k):
        return lax.rem(row + lax.div(k, side), 2) * side + lax.rem(
            col + side - lax.rem(k, side), side
        )

    def group_of(s):
        return lax.rem(s + flip, groups)

    def to_ctx(s):
        return {"ctx": half * groups + s}

    def following():
        return {"ctx": across, "seq": jnp.where(role == 1, sq + 1, sq)}

    def preceding():
        return {"ctx": across, "seq": jnp.where(role == 2, sq - 1, sq)}

    def carrier():
        return {
            "ctx": jnp.where(half == 1, me, across),
            "seq": 2 * block - 1,
        }

    def receiver(r):
        return {"ctx": me if r % 2 == 1 else across, "seq": 2 * block + 2 + r // 2}

    loads = (
        pltpu.make_async_copy(x_hbm, xv, load_sem.at[0]),
        pltpu.make_async_copy(b_hbm, bv, load_sem.at[1]),
        pltpu.make_async_copy(c_hbm, cv, load_sem.at[2]),
    )
    for load in loads:
        load.start()

    barrier = pltpu.get_barrier_semaphore()

    def greet(k, carry):
        pl.semaphore_signal(barrier, inc=1, device_id=to_ctx(partner(k)))
        return carry

    lax.fori_loop(1, groups, greet, 0)

    @pl.when(role > 0)
    def _():
        pl.semaphore_signal(barrier, inc=1, device_id=preceding())

    @pl.when(role < 3)
    def _():
        pl.semaphore_signal(barrier, inc=1, device_id=following())

    @pl.when(block > 0)
    def _():
        pl.semaphore_signal(barrier, inc=1, device_id=carrier())

    @pl.when((role == 3) & inner_x)
    def _():
        for r in range(4):
            pl.semaphore_signal(barrier, inc=1, device_id=receiver(r))

    friends = (
        groups
        - 1
        + jnp.where(role > 0, 1, 0)
        + jnp.where(role < 3, 1, 0)
        + jnp.where(block > 0, 1, 0)
        + jnp.where((role == 3) & inner_x, 4, 0)
    )
    pl.semaphore_wait(barrier, friends)

    def columns(start, size):
        return pl.ds(pl.multiple_of(start, 128), size)

    def send_group(src, dst, send_sem, recv_sem):
        def one(k, carry):
            peer = partner(k)
            pltpu.make_async_remote_copy(
                src_ref=src.at[:, columns(group_of(peer) * N, N)],
                dst_ref=dst.at[span],
                send_sem=send_sem,
                recv_sem=recv_sem,
                device_id=to_ctx(peer),
            ).start()
            return carry

        lax.fori_loop(1, groups, one, 0)

    def send_x(c):
        def one(k, carry):
            peer = partner(k)
            pltpu.make_async_remote_copy(
                src_ref=xw.at[:, columns(group_of(peer) * gw + c * cw, cw)],
                dst_ref=rx.at[c, span],
                send_sem=sx_sem.at[c],
                recv_sem=rx_sem.at[c],
                device_id=to_ctx(peer),
            ).start()
            return carry

        lax.fori_loop(1, groups, one, 0)
        pltpu.make_async_copy(
            xw.at[:, columns(mine * gw + c * cw, cw)], rx.at[c, span], rx_sem.at[c]
        ).start()

    send_group(b_hbm, rb, sb_sem, rb_sem)

    v = step_ref[...].astype(f32) + bias_ref[...]
    dt = jnp.maximum(v, 0.0) + jnp.log1p(jnp.exp(-jnp.abs(v)))
    rate = dt * (-jnp.exp(dlog_ref[...]))
    rows = lax.broadcasted_iota(jnp.int32, (tok, tok), 0)
    cols = lax.broadcasted_iota(jnp.int32, (tok, tok), 1)
    tri = (rows >= cols).astype(f32)
    cum = jnp.dot(tri, rate, precision=lax.Precision.HIGHEST, preferred_element_type=f32)
    w = dt * jnp.exp(-cum)
    ec = jnp.exp(cum)
    w_hi = w.astype(bf16)
    w_lo = (w - w_hi.astype(f32)).astype(bf16)
    e_hi = ec.astype(bf16)
    e_lo = (ec - e_hi.astype(f32)).astype(bf16)
    gain = jnp.broadcast_to(gain_ref[...], (16, heads))
    g_hi = gain.astype(bf16)
    g_lo = (gain - g_hi.astype(f32)).astype(bf16)
    for g in range(groups):
        part_of = slice(g * share, (g + 1) * share)
        w2[g, :, :share] = w_hi[:, part_of]
        w2[g, :, share:] = w_lo[:, part_of]
        ec2[g, :tok, :share] = e_hi[:, part_of]
        ec2[g, :tok, share:] = e_lo[:, part_of]
        ec2[g, tok:, :share] = g_hi[:, part_of]
        ec2[g, tok:, share:] = g_lo[:, part_of]
    slot_of = lax.broadcasted_iota(jnp.int32, (2 * share, gw), 0)
    lane_of = lax.broadcasted_iota(jnp.int32, (2 * share, gw), 1)
    spread[...] = jnp.where(lax.rem(slot_of, share) == lax.div(lane_of, P_SIZE), 1.0, 0.0).astype(bf16)

    loads[0].wait()

    def weigh(c):
        def one(g, carry):
            at = columns(g * gw + c * cw, cw)
            weight = jnp.dot(w2[g], spread[:, c * cw : (c + 1) * cw], preferred_element_type=f32)
            xw[:, at] = (xv[:, at].astype(f32) * weight).astype(bf16)
            return carry

        lax.fori_loop(0, groups, one, 0)

    weigh(0)
    send_x(0)

    ends = lax.dot_general(
        rate,
        jnp.ones((tok, 128), f32),
        (((0,), (0,)), ((), ())),
        precision=lax.Precision.HIGHEST,
        preferred_element_type=f32,
    )
    head_of = lax.broadcasted_iota(jnp.int32, (heads, 128), 0)
    half_of = lax.div(lax.broadcasted_iota(jnp.int32, (heads, 128), 1), P_SIZE)
    halves = jnp.where(lax.rem(head_of, 2) == half_of, jnp.exp(ends), 0.0)
    pair_row = lax.broadcasted_iota(jnp.int32, (heads // 2, heads), 0)
    pair_col = lax.div(lax.broadcasted_iota(jnp.int32, (heads // 2, heads), 1), 2)
    pick = (pair_row == pair_col).astype(f32)
    tiles = jnp.dot(pick, halves, precision=lax.Precision.HIGHEST, preferred_element_type=f32)
    dsend[...] = tiles.reshape(groups, gw // 128, 128)

    def send_d(k, carry):
        peer = partner(k)
        pltpu.make_async_remote_copy(
            src_ref=dsend.at[group_of(peer)],
            dst_ref=rd.at[span],
            send_sem=sd_sem,
            recv_sem=rd_sem,
            device_id=to_ctx(peer),
        ).start()
        return carry

    lax.fori_loop(1, groups, send_d, 0)
    pltpu.make_async_copy(dsend.at[mine], rd.at[span], rd_sem).start()
    for c in range(1, CHUNKS):
        weigh(c)
        send_x(c)
        if c == 2:
            send_group(c_hbm, rc, sc_sem, rc_sem)

    loads[1].wait()
    loads[2].wait()
    own = columns(mine * N, N)
    pltpu.make_async_copy(bv.at[:, own], rb.at[span], rb_sem).start()
    pltpu.make_async_copy(cv.at[:, own], rc.at[span], rc_sem).start()

    @pl.when(role == 0)
    def _():
        pre[...] = jnp.zeros(pre.shape, bf16)
        pre_d[...] = jnp.ones(pre_d.shape, f32)

    @pl.when(block == 0)
    def _():
        head[...] = jnp.zeros(head.shape, bf16)

    def local_part(g):
        at = slice(g * gw, (g + 1) * gw)
        state_at = slice(g * N, (g + 1) * N)
        inner = lax.dot_general(
            cv[:, state_at], bv[:, state_at], (((1,), (1,)), ((), ())), preferred_element_type=f32
        )
        inner = jnp.where(rows >= cols, inner, 0.0).astype(bf16)

        def one(c, carry):
            at = columns(g * gw + c * cw, cw)
            diag = jnp.dot(inner, xw[:, at], preferred_element_type=f32)
            scale = jnp.dot(ec2[g], spread[:, columns(c * cw, cw)], preferred_element_type=f32)
            part[:, at] = scale[:tok] * diag + scale[tok : tok + 1] * xv[:, at].astype(f32)
            return carry

        lax.fori_loop(0, CHUNKS, one, 0)

    def decay_row(c, s):
        per = cw // 128
        tile = rd[s]
        return jnp.concatenate([tile[c * per + r : c * per + r + 1] for r in range(per)], axis=1)

    def gather_states(c):
        pltpu.make_async_copy(rx.at[c], rx.at[c], rx_sem.at[c]).wait()
        slot = c % SLOTS
        total[c] = jnp.zeros(total.shape[1:], f32)

        def one(s, product):
            piece = lax.dot_general(
                rb[s], rx[c, s], (((0,), (0,)), ((), ())), preferred_element_type=f32
            )
            factor = decay_row(c, s)
            states[slot, s] = piece
            total[c] = factor * (total[c] + piece)
            return product * factor

        whole[c] = lax.fori_loop(0, groups, one, jnp.ones((1, cw), f32))

    def pass_run(c):
        return (
            pltpu.make_async_remote_copy(
                src_ref=run.at[c],
                dst_ref=pre.at[c],
                send_sem=sr_sem.at[c],
                recv_sem=rr_sem.at[c],
                device_id=following(),
            ),
            pltpu.make_async_remote_copy(
                src_ref=run_d.at[c],
                dst_ref=pre_d.at[c],
                send_sem=srd_sem.at[c],
                recv_sem=rrd_sem.at[c],
                device_id=following(),
            ),
        )

    def pass_head(c, r):
        return pltpu.make_async_remote_copy(
            src_ref=nexthead.at[c],
            dst_ref=head.at[c],
            send_sem=sh_sem.at[c, r],
            recv_sem=rh_sem.at[c],
            device_id=receiver(r),
        )

    def compose(c):
        @pl.when(role > 0)
        def _():
            for copy in pass_run(c):
                copy.wait_recv()

        ahead = whole[c] * pre[c].astype(f32) + total[c]
        span_d = whole[c] * pre_d[c, :1]

        @pl.when(role < 3)
        def _():
            run[c] = ahead.astype(bf16)
            run_d[c] = jnp.broadcast_to(span_d, run_d.shape[1:])
            for copy in pass_run(c):
                copy.start()

        @pl.when((role == 3) & inner_x)
        def _():
            total[c] = ahead
            whole[c] = span_d

    def forward(c):
        @pl.when((role == 3) & inner_x)
        def _():
            @pl.when(block > 0)
            def _():
                pass_head(c, 0).wait_recv()

            nexthead[c] = (whole[c] * head[c].astype(f32) + total[c]).astype(bf16)
            for r in (3, 2, 1, 0):
                pass_head(c, r).start()

    def read_states(c):
        @pl.when((block > 0) & ((role < 3) | (block == blocks - 1)))
        def _():
            pass_head(c, 0).wait_recv()

        slot = c % SLOTS
        entry[...] = pre_d[c, :1] * head[c].astype(f32) + pre[c].astype(f32)

        def one(s, carry):
            state = entry[...]
            offs[c, s] = jnp.dot(rc[s], state.astype(bf16), preferred_element_type=f32).astype(bf16)
            entry[...] = decay_row(c, s) * (state + states[slot, s])
            return carry

        lax.fori_loop(0, groups, one, 0)
        at = columns(mine * gw + c * cw, cw)

        def send(k, carry):
            peer = partner(k)
            pltpu.make_async_remote_copy(
                src_ref=offs.at[c, peer],
                dst_ref=offr.at[:, at],
                send_sem=so_sem.at[c],
                recv_sem=ro_sem.at[c, span],
                device_id=to_ctx(peer),
            ).start()
            return carry

        lax.fori_loop(1, groups, send, 0)
        pltpu.make_async_copy(offs.at[c, span], offr.at[:, at], ro_sem.at[c, span]).start()

    def combine(c):
        def one(k, carry):
            s = source(k)
            g = group_of(s)
            at = columns(g * gw + c * cw, cw)
            pltpu.make_async_copy(offs.at[c, 0], offr.at[:, at], ro_sem.at[c, s]).wait()
            scale = jnp.dot(
                ec2[g, :tok, :], spread[:, c * cw : (c + 1) * cw], preferred_element_type=f32
            )
            o_ref[:, at] = (part[:, at] + scale * offr[:, at].astype(f32)).astype(bf16)
            return carry

        lax.fori_loop(0, groups, one, 0)

    pltpu.make_async_copy(rb, rb, rb_sem).wait()
    pltpu.make_async_copy(rd, rd, rd_sem).wait()
    lag = SLOTS - 1
    for c in range(CHUNKS + lag):
        if c < CHUNKS:
            gather_states(c)
            compose(c)
            forward(c)
        if c == lag:
            pltpu.make_async_copy(rc, rc, rc_sem).wait()
        if c >= lag:
            read_states(c - lag)
        if c < groups:
            local_part(c)
    for c in range(CHUNKS):
        combine(c)

    for c in range(CHUNKS):
        pltpu.make_async_copy(rx.at[c, 1:], rx.at[c, 1:], sx_sem.at[c]).wait()
        pltpu.make_async_copy(offs.at[c, 1:], offs.at[c, 1:], so_sem.at[c]).wait()

        @pl.when(role < 3)
        def _():
            for copy in pass_run(c):
                copy.wait_send()

        @pl.when((role == 3) & inner_x)
        def _():
            for r in range(4):
                pass_head(c, r).wait_send()

    pltpu.make_async_copy(rb.at[1:], rb.at[1:], sb_sem).wait()
    pltpu.make_async_copy(rc.at[1:], rc.at[1:], sc_sem).wait()
    pltpu.make_async_copy(rd.at[1:], rd.at[1:], sd_sem).wait()


def body(mixer_input, step_raw, b_proj, c_proj, step_bias, decay_log, skip_gain):
    nc, ns = lax.axis_size("ctx"), lax.axis_size("seq")
    tok, width = mixer_input.shape
    heads = step_raw.shape[1]
    groups = b_proj.shape[1] // N
    share = heads // groups
    gw = share * P_SIZE
    cw = gw // CHUNKS
    f32, bf16 = jnp.float32, jnp.bfloat16
    any_spec = pl.BlockSpec(memory_space=pl.ANY)
    vmem_spec = pl.BlockSpec(memory_space=pltpu.VMEM)
    dma = pltpu.SemaphoreType.DMA
    return pl.pallas_call(
        functools.partial(scan_kernel, nc, ns, groups),
        out_shape=pltpu.VMEM((tok, width), bf16),
        in_specs=[any_spec, vmem_spec, any_spec, any_spec, vmem_spec, vmem_spec, vmem_spec],
        out_specs=vmem_spec,
        scratch_shapes=[
            pltpu.VMEM((tok, width), bf16),
            pltpu.VMEM((tok, groups * N), bf16),
            pltpu.VMEM((tok, groups * N), bf16),
            pltpu.VMEM((tok, width), bf16),
            pltpu.VMEM((2 * share, gw), bf16),
            pltpu.VMEM((groups, tok, 2 * share), bf16),
            pltpu.VMEM((groups, tok + 16, 2 * share), bf16),
            pltpu.VMEM((groups, gw // 128, 128), f32),
            pltpu.VMEM((groups, tok, N), bf16),
            pltpu.VMEM((groups, tok, N), bf16),
            pltpu.VMEM((CHUNKS, groups, tok, cw), bf16),
            pltpu.VMEM((groups, gw // 128, 128), f32),
            pltpu.VMEM((SLOTS, groups, N, cw), f32),
            pltpu.VMEM((CHUNKS, N, cw), f32),
            pltpu.VMEM((CHUNKS, 1, cw), f32),
            pltpu.VMEM((N, cw), f32),
            pltpu.VMEM((CHUNKS, N, cw), bf16),
            pltpu.VMEM((CHUNKS, 8, cw), f32),
            pltpu.VMEM((CHUNKS, N, cw), bf16),
            pltpu.VMEM((CHUNKS, 8, cw), f32),
            pltpu.VMEM((CHUNKS, N, cw), bf16),
            pltpu.VMEM((CHUNKS, N, cw), bf16),
            pltpu.VMEM((CHUNKS, groups, tok, cw), bf16),
            pltpu.VMEM((tok, width), bf16),
            pltpu.VMEM((tok, width), f32),
            dma((3,)),
            dma,
            dma,
            dma,
            dma((CHUNKS,)),
            dma((CHUNKS,)),
            dma((CHUNKS,)),
            dma((CHUNKS,)),
            dma((CHUNKS, 4)),
            dma,
            dma,
            dma,
            dma((CHUNKS,)),
            dma((CHUNKS, groups)),
            dma((CHUNKS,)),
            dma((CHUNKS,)),
            dma((CHUNKS,)),
        ],
        compiler_params=pltpu.CompilerParams(
            collective_id=0, has_side_effects=True, vmem_limit_bytes=56 * 1024 * 1024
        ),
    )(
        mixer_input,
        step_raw,
        b_proj,
        c_proj,
        step_bias.reshape(1, heads),
        decay_log.reshape(1, heads),
        skip_gain.reshape(1, heads),
    )


def solution(mesh):
    return jax.shard_map(
        body,
        mesh=mesh,
        in_specs=(
            P(("seq", "ctx"), None),
            P(("seq", "ctx"), None),
            P(("seq", "ctx"), None),
            P(("seq", "ctx"), None),
            P(),
            P(),
            P(),
        ),
        out_specs=P(("seq", "ctx"), None),
        check_vma=False,
    )
```

time: 147 us -> 116 us (0.79)
  the two profiles are of different devices: /device:TPU:119 before, /device:TPU:2 now
where the time goes in v3:
time: 116 us
  Pallas kernels  114 us (98%)
  local copies, waits for them, and re-layouts  2.02 us (2%)
    pallas_call x1, Pallas kernels, body(): pl.pallas_call(functools.partial(scan_kernel, nc, ns, groups), out_shape=...  114 us

profile of v3, /device:TPU:2, one launch (start us, length us, event | category | flops | bytes accessed | tf_op | source)
XLA Modules:
  0.0 115.6 jit_solution(15800774472763215879)
XLA Ops:
  0.0 113.6 %shard_map.73 = bf16[128,16384]{1,0:T(8,128)(2,1)S(1)} custom-call(bf16[128,16384]{1,0:T(8,128)(2,1)} %x_hbm.1, bf16[128,256]{1,0:T(8,128)(2,1)} %step_ref.1, bf16[128,2048]{1,0:T(8,128)(2,1)} %b_hbm.1, bf16[128,2048]{1,0:T(8,128)(2,1)} %c_hbm.1, f32[1,256]{1,0:T(1,128)} %bitcast.3, f32[1,256]{1,0:T(1,128)} %bitcast.4, f32[1,256]{1,0:T(1,128)} %bitcast.5), custom_call_target="tpu_custom_call" | custom-call | tf_op jit(solution)/shard_map/pallas_call | solution.py:480
  113.6 2.0 %copy.9 = bf16[128,16384]{1,0:T(8,128)(2,1)} copy(bf16[128,16384]{1,0:T(8,128)(2,1)S(1)} %shard_map.73) | data formatting | bytes 8388608

commit v4 on v3

--- a/solution.py
+++ b/solution.py
@@ -18,13 +18,17 @@
     ns,
     groups,
     x_hbm,
-    step_ref,
+    step_hbm,
     b_hbm,
     c_hbm,
+    bias_hbm,
+    dlog_hbm,
+    gain_hbm,
+    o_ref,
+    step_ref,
     bias_ref,
     dlog_ref,
     gain_ref,
-    o_ref,
     xv,
     bv,
     cv,
@@ -37,6 +41,7 @@
     rc,
     rx,
     rd,
+    wide_d,
     states,
     total,
     whole,
@@ -116,38 +121,42 @@
     def receiver(r):
         return {"ctx": me if r % 2 == 1 else across, "seq": 2 * block + 2 + r // 2}
 
+    barrier = pltpu.get_barrier_semaphore()
+
+    def greet(k, carry):
+        pl.semaphore_signal(barrier, inc=1, device_id=to_ctx(partner(k)))
+        return carry
+
+    lax.fori_loop(1, groups, greet, 0)
+
+    @pl.when(role > 0)
+    def _():
+        pl.semaphore_signal(barrier, inc=1, device_id=preceding())
+
+    @pl.when(role < 3)
+    def _():
+        pl.semaphore_signal(barrier, inc=1, device_id=following())
+
+    @pl.when(block > 0)
+    def _():
+        pl.semaphore_signal(barrier, inc=1, device_id=carrier())
+
+    @pl.when((role == 3) & inner_x)
+    def _():
+        for r in range(4):
+            pl.semaphore_signal(barrier, inc=1, device_id=receiver(r))
+
     loads = (
         pltpu.make_async_copy(x_hbm, xv, load_sem.at[0]),
         pltpu.make_async_copy(b_hbm, bv, load_sem.at[1]),
         pltpu.make_async_copy(c_hbm, cv, load_sem.at[2]),
+        pltpu.make_async_copy(step_hbm, step_ref, load_sem.at[3]),
+        pltpu.make_async_copy(bias_hbm, bias_ref, load_sem.at[4]),
+        pltpu.make_async_copy(dlog_hbm, dlog_ref, load_sem.at[5]),
+        pltpu.make_async_copy(gain_hbm, gain_ref, load_sem.at[6]),
     )
-    for load in loads:
+    for load in loads[3:] + loads[:3]:
         load.start()
-
-    barrier = pltpu.get_barrier_semaphore()
-
-    def greet(k, carry):
-        pl.semaphore_signal(barrier, inc=1, device_id=to_ctx(partner(k)))
-        return carry
-
-    lax.fori_loop(1, groups, greet, 0)
-
-    @pl.when(role > 0)
-    def _():
-        pl.semaphore_signal(barrier, inc=1, device_id=preceding())
-
-    @pl.when(role < 3)
-    def _():
-        pl.semaphore_signal(barrier, inc=1, device_id=following())
-
-    @pl.when(block > 0)
-    def _():
-        pl.semaphore_signal(barrier, inc=1, device_id=carrier())
-
-    @pl.when((role == 3) & inner_x)
-    def _():
-        for r in range(4):
-            pl.semaphore_signal(barrier, inc=1, device_id=receiver(r))
 
     friends = (
         groups
@@ -164,7 +173,7 @@
 
     def send_group(src, dst, send_sem, recv_sem):
         def one(k, carry):
-            peer = partner(k)
+            peer = partner(groups - k)
             pltpu.make_async_remote_copy(
                 src_ref=src.at[:, columns(group_of(peer) * N, N)],
                 dst_ref=dst.at[span],
@@ -178,7 +187,7 @@
 
     def send_x(c):
         def one(k, carry):
-            peer = partner(k)
+            peer = partner(groups - k)
             pltpu.make_async_remote_copy(
                 src_ref=xw.at[:, columns(group_of(peer) * gw + c * cw, cw)],
                 dst_ref=rx.at[c, span],
@@ -195,6 +204,8 @@
 
     send_group(b_hbm, rb, sb_sem, rb_sem)
 
+    for load in loads[3:]:
+        load.wait()
     v = step_ref[...].astype(f32) + bias_ref[...]
     dt = jnp.maximum(v, 0.0) + jnp.log1p(jnp.exp(-jnp.abs(v)))
     rate = dt * (-jnp.exp(dlog_ref[...]))
@@ -211,6 +222,7 @@
     gain = jnp.broadcast_to(gain_ref[...], (16, heads))
     g_hi = gain.astype(bf16)
     g_lo = (gain - g_hi.astype(f32)).astype(bf16)
+    dsend[...] = jnp.zeros(dsend.shape, f32)
     for g in range(groups):
         part_of = slice(g * share, (g + 1) * share)
         w2[g, :, :share] = w_hi[:, part_of]
@@ -219,6 +231,7 @@
         ec2[g, :tok, share:] = e_lo[:, part_of]
         ec2[g, tok:, :share] = g_hi[:, part_of]
         ec2[g, tok:, share:] = g_lo[:, part_of]
+        dsend[g, :, :share] = ec[tok - 1 :, part_of]
     slot_of = lax.broadcasted_iota(jnp.int32, (2 * share, gw), 0)
     lane_of = lax.broadcasted_iota(jnp.int32, (2 * share, gw), 1)
     spread[...] = jnp.where(lax.rem(slot_of, share) == lax.div(lane_of, P_SIZE), 1.0, 0.0).astype(bf16)
@@ -237,24 +250,8 @@
     weigh(0)
     send_x(0)
 
-    ends = lax.dot_general(
-        rate,
-        jnp.ones((tok, 128), f32),
-        (((0,), (0,)), ((), ())),
-        precision=lax.Precision.HIGHEST,
-        preferred_element_type=f32,
-    )
-    head_of = lax.broadcasted_iota(jnp.int32, (heads, 128), 0)
-    half_of = lax.div(lax.broadcasted_iota(jnp.int32, (heads, 128), 1), P_SIZE)
-    halves = jnp.where(lax.rem(head_of, 2) == half_of, jnp.exp(ends), 0.0)
-    pair_row = lax.broadcasted_iota(jnp.int32, (heads // 2, heads), 0)
-    pair_col = lax.div(lax.broadcasted_iota(jnp.int32, (heads // 2, heads), 1), 2)
-    pick = (pair_row == pair_col).astype(f32)
-    tiles = jnp.dot(pick, halves, precision=lax.Precision.HIGHEST, preferred_element_type=f32)
-    dsend[...] = tiles.reshape(groups, gw // 128, 128)
-
     def send_d(k, carry):
-        peer = partner(k)
+        peer = partner(groups - k)
         pltpu.make_async_remote_copy(
             src_ref=dsend.at[group_of(peer)],
             dst_ref=rd.at[span],
@@ -269,7 +266,7 @@
     for c in range(1, CHUNKS):
         weigh(c)
         send_x(c)
-        if c == 2:
+        if c == 4:
             send_group(c_hbm, rc, sc_sem, rc_sem)
 
     loads[1].wait()
@@ -293,21 +290,32 @@
         inner = lax.dot_general(
             cv[:, state_at], bv[:, state_at], (((1,), (1,)), ((), ())), preferred_element_type=f32
         )
-        inner = jnp.where(rows >= cols, inner, 0.0).astype(bf16)
+        inner = jnp.where(rows >= cols, inner, 0.0)
+        top = inner.astype(bf16)
+        rest = (inner - top.astype(f32)).astype(bf16)
 
         def one(c, carry):
             at = columns(g * gw + c * cw, cw)
-            diag = jnp.dot(inner, xw[:, at], preferred_element_type=f32)
+            diag = jnp.dot(top, xw[:, at], preferred_element_type=f32)
+            diag += jnp.dot(rest, xw[:, at], preferred_element_type=f32)
             scale = jnp.dot(ec2[g], spread[:, columns(c * cw, cw)], preferred_element_type=f32)
             part[:, at] = scale[:tok] * diag + scale[tok : tok + 1] * xv[:, at].astype(f32)
             return carry
 
         lax.fori_loop(0, CHUNKS, one, 0)
 
+    def widen_decays():
+        left = jnp.concatenate([rd[s] for s in range(groups)], axis=0)[:, :share]
+        wide = jnp.zeros((groups, gw), f32)
+        for _ in range(3):
+            term = left.astype(bf16)
+            left = left - term.astype(f32)
+            wide = wide + jnp.dot(term, spread[:share], preferred_element_type=f32)
+        for s in range(groups):
+            wide_d[s] = wide[s : s + 1]
+
     def decay_row(c, s):
-        per = cw // 128
-        tile = rd[s]
-        return jnp.concatenate([tile[c * per + r : c * per + r + 1] for r in range(per)], axis=1)
+        return wide_d[s, :, c * cw : (c + 1) * cw]
 
     def gather_states(c):
         pltpu.make_async_copy(rx.at[c], rx.at[c], rx_sem.at[c]).wait()
@@ -402,7 +410,7 @@
         at = columns(mine * gw + c * cw, cw)
 
         def send(k, carry):
-            peer = partner(k)
+            peer = partner(groups - k)
             pltpu.make_async_remote_copy(
                 src_ref=offs.at[c, peer],
                 dst_ref=offr.at[:, at],
@@ -417,7 +425,7 @@
 
     def combine(c):
         def one(k, carry):
-            s = source(k)
+            s = source(lax.rem(groups - k, groups))
             g = group_of(s)
             at = columns(g * gw + c * cw, cw)
             pltpu.make_async_copy(offs.at[c, 0], offr.at[:, at], ro_sem.at[c, s]).wait()
@@ -431,6 +439,7 @@
 
     pltpu.make_async_copy(rb, rb, rb_sem).wait()
     pltpu.make_async_copy(rd, rd, rd_sem).wait()
+    widen_decays()
     lag = SLOTS - 1
     for c in range(CHUNKS + lag):
         if c < CHUNKS:
@@ -480,9 +489,13 @@
     return pl.pallas_call(
         functools.partial(scan_kernel, nc, ns, groups),
         out_shape=pltpu.VMEM((tok, width), bf16),
-        in_specs=[any_spec, vmem_spec, any_spec, any_spec, vmem_spec, vmem_spec, vmem_spec],
+        in_specs=[any_spec] * 7,
         out_specs=vmem_spec,
         scratch_shapes=[
+            pltpu.VMEM((tok, heads), bf16),
+            pltpu.VMEM((1, heads), f32),
+            pltpu.VMEM((1, heads), f32),
+            pltpu.VMEM((1, heads), f32),
             pltpu.VMEM((tok, width), bf16),
             pltpu.VMEM((tok, groups * N), bf16),
             pltpu.VMEM((tok, groups * N), bf16),
@@ -490,11 +503,12 @@
             pltpu.VMEM((2 * share, gw), bf16),
             pltpu.VMEM((groups, tok, 2 * share), bf16),
             pltpu.VMEM((groups, tok + 16, 2 * share), bf16),
-            pltpu.VMEM((groups, gw // 128, 128), f32),
+            pltpu.VMEM((groups, 1, 128), f32),
             pltpu.VMEM((groups, tok, N), bf16),
             pltpu.VMEM((groups, tok, N), bf16),
             pltpu.VMEM((CHUNKS, groups, tok, cw), bf16),
-            pltpu.VMEM((groups, gw // 128, 128), f32),
+            pltpu.VMEM((groups, 1, 128), f32),
+            pltpu.VMEM((groups, 1, gw), f32),
             pltpu.VMEM((SLOTS, groups, N, cw), f32),
             pltpu.VMEM((CHUNKS, N, cw), f32),
             pltpu.VMEM((CHUNKS, 1, cw), f32),
@@ -508,7 +522,7 @@
             pltpu.VMEM((CHUNKS, groups, tok, cw), bf16),
             pltpu.VMEM((tok, width), bf16),
             pltpu.VMEM((tok, width), f32),
-            dma((3,)),
+            dma((7,)),
             dma,
             dma,
             dma,

time: 116 us -> 114 us (0.983)
  Pallas kernels: 114 us -> 111 us
    pallas_call x1, Pallas kernels: 114 us -> 111 us  [body(): pl.pallas_call(functools.partial(scan_kernel, nc, ns, groups), out_shape=...]
where the time goes in v4:
time: 114 us; the launch traced here: 113 us
  Pallas kernels  111 us (97%)
  local copies, waits for them, and re-layouts  2.02 us (2%)
    pallas_call x1, Pallas kernels, body(): pl.pallas_call(functools.partial(scan_kernel, nc, ns, groups), out_shape=...  111 us

profile of v4, /device:TPU:2, one launch (start us, length us, event | category | flops | bytes accessed | tf_op | source)
XLA Modules:
  0.0 113.2 jit_solution(6802894311738933919)
XLA Ops:
  0.0 111.2 %shard_map.73 = bf16[128,16384]{1,0:T(8,128)(2,1)S(1)} custom-call(bf16[128,16384]{1,0:T(8,128)(2,1)} %x_hbm.1, bf16[128,256]{1,0:T(8,128)(2,1)} %step_hbm.1, bf16[128,2048]{1,0:T(8,128)(2,1)} %b_hbm.1, bf16[128,2048]{1,0:T(8,128)(2,1)} %c_hbm.1, f32[1,256]{1,0:T(1,128)} %bitcast.3, f32[1,256]{1,0:T(1,128)} %bitcast.4, f32[1,256]{1,0:T(1,128)} %bitcast.5), custom_call_target="tpu_custom_call" | custom-call | tf_op jit(solution)/shard_map/pallas_call | solution.py:489
  111.2 2.0 %copy.9 = bf16[128,16384]{1,0:T(8,128)(2,1)} copy(bf16[128,16384]{1,0:T(8,128)(2,1)S(1)} %shard_map.73) | data formatting | bytes 8388608

commit v5 on v4

--- a/solution.py
+++ b/solution.py
@@ -363,8 +363,8 @@
     def compose(c):
         @pl.when(role > 0)
         def _():
-            for copy in pass_run(c):
-                copy.wait_recv()
+            pltpu.make_async_copy(pre.at[c], pre.at[c], rr_sem.at[c]).wait()
+            pltpu.make_async_copy(pre_d.at[c], pre_d.at[c], rrd_sem.at[c]).wait()
 
         ahead = whole[c] * pre[c].astype(f32) + total[c]
         span_d = whole[c] * pre_d[c, :1]
@@ -386,7 +386,7 @@
         def _():
             @pl.when(block > 0)
             def _():
-                pass_head(c, 0).wait_recv()
+                pltpu.make_async_copy(head.at[c], head.at[c], rh_sem.at[c]).wait()
 
             nexthead[c] = (whole[c] * head[c].astype(f32) + total[c]).astype(bf16)
             for r in (3, 2, 1, 0):
@@ -395,7 +395,7 @@
     def read_states(c):
         @pl.when((block > 0) & ((role < 3) | (block == blocks - 1)))
         def _():
-            pass_head(c, 0).wait_recv()
+            pltpu.make_async_copy(head.at[c], head.at[c], rh_sem.at[c]).wait()
 
         slot = c % SLOTS
         entry[...] = pre_d[c, :1] * head[c].astype(f32) + pre[c].astype(f32)

time: 114 us -> 114 us (level)
  no operation moved by 1% of the time
where the time goes in v5:
time: 114 us; the launch traced here: 113 us
  Pallas kernels  111 us (97%)
  local copies, waits for them, and re-layouts  2.02 us (2%)
    pallas_call x1, Pallas kernels, body(): pl.pallas_call(functools.partial(scan_kernel, nc, ns, groups), out_shape=...  111 us

profile of v5, /device:TPU:2, one launch (start us, length us, event | category | flops | bytes accessed | tf_op | source)
XLA Modules:
  0.0 113.2 jit_solution(6802894311738933919)
XLA Ops:
  0.0 111.2 %shard_map.73 = bf16[128,16384]{1,0:T(8,128)(2,1)S(1)} custom-call(bf16[128,16384]{1,0:T(8,128)(2,1)} %x_hbm.1, bf16[128,256]{1,0:T(8,128)(2,1)} %step_hbm.1, bf16[128,2048]{1,0:T(8,128)(2,1)} %b_hbm.1, bf16[128,2048]{1,0:T(8,128)(2,1)} %c_hbm.1, f32[1,256]{1,0:T(1,128)} %bitcast.3, f32[1,256]{1,0:T(1,128)} %bitcast.4, f32[1,256]{1,0:T(1,128)} %bitcast.5), custom_call_target="tpu_custom_call" | custom-call | tf_op jit(solution)/shard_map/pallas_call | solution.py:489
  111.2 2.0 %copy.9 = bf16[128,16384]{1,0:T(8,128)(2,1)} copy(bf16[128,16384]{1,0:T(8,128)(2,1)S(1)} %shard_map.73) | data formatting | bytes 8388608

commit v6 on v5

--- a/solution.py
+++ b/solution.py
@@ -266,7 +266,7 @@
     for c in range(1, CHUNKS):
         weigh(c)
         send_x(c)
-        if c == 4:
+        if c == 3:
             send_group(c_hbm, rc, sc_sem, rc_sem)
 
     loads[1].wait()

time: 114 us -> 114 us (level)
  no operation moved by 1% of the time
where the time goes in v6:
time: 114 us; the launch traced here: 113 us
  Pallas kernels  111 us (97%)
  local copies, waits for them, and re-layouts  2.02 us (2%)
    pallas_call x1, Pallas kernels, body(): pl.pallas_call(functools.partial(scan_kernel, nc, ns, groups), out_shape=...  111 us

profile of v6, /device:TPU:2, one launch (start us, length us, event | category | flops | bytes accessed | tf_op | source)
XLA Modules:
  0.0 113.2 jit_solution(13828128866010022342)
XLA Ops:
  0.0 111.2 %shard_map.73 = bf16[128,16384]{1,0:T(8,128)(2,1)S(1)} custom-call(bf16[128,16384]{1,0:T(8,128)(2,1)} %x_hbm.1, bf16[128,256]{1,0:T(8,128)(2,1)} %step_hbm.1, bf16[128,2048]{1,0:T(8,128)(2,1)} %b_hbm.1, bf16[128,2048]{1,0:T(8,128)(2,1)} %c_hbm.1, f32[1,256]{1,0:T(1,128)} %bitcast.3, f32[1,256]{1,0:T(1,128)} %bitcast.4, f32[1,256]{1,0:T(1,128)} %bitcast.5), custom_call_target="tpu_custom_call" | custom-call | tf_op jit(solution)/shard_map/pallas_call | solution.py:489
  111.2 2.0 %copy.9 = bf16[128,16384]{1,0:T(8,128)(2,1)} copy(bf16[128,16384]{1,0:T(8,128)(2,1)S(1)} %shard_map.73) | data formatting | bytes 8388608

commit v7 on v5

--- a/solution.py
+++ b/solution.py
@@ -452,7 +452,9 @@
             read_states(c - lag)
         if c < groups:
             local_part(c)
-    for c in range(CHUNKS):
+        if c >= CHUNKS:
+            combine(c - CHUNKS)
+    for c in range(lag, CHUNKS):
         combine(c)
 
     for c in range(CHUNKS):

time: 114 us -> 114 us (level)
  no operation moved by 1% of the time
where the time goes in v7:
time: 114 us; the launch traced here: 113 us
  Pallas kernels  111 us (97%)
  local copies, waits for them, and re-layouts  2.02 us (2%)
    pallas_call x1, Pallas kernels, body(): pl.pallas_call(functools.partial(scan_kernel, nc, ns, groups), out_shape=...  111 us

profile of v7, /device:TPU:2, one launch (start us, length us, event | category | flops | bytes accessed | tf_op | source)
XLA Modules:
  0.0 113.2 jit_solution(14671312992921869015)
XLA Ops:
  0.0 111.2 %shard_map.73 = bf16[128,16384]{1,0:T(8,128)(2,1)S(1)} custom-call(bf16[128,16384]{1,0:T(8,128)(2,1)} %x_hbm.1, bf16[128,256]{1,0:T(8,128)(2,1)} %step_hbm.1, bf16[128,2048]{1,0:T(8,128)(2,1)} %b_hbm.1, bf16[128,2048]{1,0:T(8,128)(2,1)} %c_hbm.1, f32[1,256]{1,0:T(1,128)} %bitcast.3, f32[1,256]{1,0:T(1,128)} %bitcast.4, f32[1,256]{1,0:T(1,128)} %bitcast.5), custom_call_target="tpu_custom_call" | custom-call | tf_op jit(solution)/shard_map/pallas_call | solution.py:491
  111.2 2.0 %copy.9 = bf16[128,16384]{1,0:T(8,128)(2,1)} copy(bf16[128,16384]{1,0:T(8,128)(2,1)S(1)} %shard_map.73) | data formatting | bytes 8388608
